TPU v7x, 128 devices: a whole 4x4x4 slice. The times are simulated.
128 devices in a mesh: rows: 16 (over y, z_lo, core), reg: 8 (over z_hi, x).
Axes of the slice: x: 4, y: 4, z: 4 (z_hi: 2, z_lo: 2; z = z_hi * 2 + z_lo), core: 2. Of those that a mesh axis runs over, the one named last changes fastest.
Arguments:
- snapshots: bfloat16 [131072, 2048], P('rows', 'reg'), may hold values from -6 to 6
- rates: bfloat16 [131072, 2048], P('rows', 'reg'), may hold values from -6 to 6
- basis: bfloat16 [131072, 128], P('rows'), may hold values from -0.015625 to 0.015625
Outputs:
- gram: float32 [8384, 8384], P('rows', 'reg')
- rhs: float32 [8384, 128], P('rows')
All inputs are finite; a program needn't handle non-finite values.
Results may differ from a plain program's by a relative error of at most 0.0042.
Values may be sent and summed in bfloat16 or wider, within the bound.
A program may use at most 64 MiB of HBM per device.

v0:
```python
import jax
import jax.numpy as jnp
import numpy as np
from jax import lax
from jax.sharding import PartitionSpec as P


def make_features(states):
    upper_i, upper_j = np.triu_indices(states.shape[0])
    quad = jnp.take(states, upper_i, axis=0) * jnp.take(states, upper_j, axis=0)
    return jnp.concatenate([states, quad], axis=0).astype(jnp.bfloat16)


def block_adder(col_feat, total, piece):
    columns = lax.slice_in_dim(col_feat, 0, piece.shape[1], axis=1)
    return total + lax.dot_general(
        piece, columns, (((1,), (1,)), ((), ())), preferred_element_type=jnp.float32
    )


def per_device(snapshots, rates, basis):
    rank = basis.shape[1]
    width = rank + rank * (rank + 1) // 2
    local_time = snapshots.shape[1]
    total_time = local_time * lax.axis_size("reg")
    row_width = width // lax.axis_size("rows")
    col_width = width // lax.axis_size("reg")
    part_states = jnp.einsum("nr,nt->rt", basis, snapshots, preferred_element_type=jnp.float32)
    part_rates = jnp.einsum("nr,nt->rt", basis, rates, preferred_element_type=jnp.float32)
    empty = jnp.zeros((row_width, col_width), jnp.float32)
    states = lax.psum_scatter(part_states, "rows", scatter_dimension=1, tiled=True)
    moments = lax.psum(part_rates, "rows")
    local_feat = make_features(states)
    row_feat = lax.all_to_all(local_feat, "rows", split_axis=0, concat_axis=1, tiled=True)
    full_feat = lax.all_gather(local_feat, "rows", axis=1, tiled=True)
    col_feat = lax.all_to_all(full_feat, "reg", split_axis=0, concat_axis=1, tiled=True)
    gram = block_adder(col_feat, empty, lax.all_gather(row_feat, "reg", axis=1, tiled=True))
    rate_half = moments.astype(jnp.bfloat16)
    rhs_part = lax.dot_general(
        row_feat, rate_half, (((1,), (1,)), ((), ())), preferred_element_type=jnp.float32
    )
    rhs = lax.psum(rhs_part, "reg")
    return (gram / float(total_time), rhs / float(total_time))


def solution(mesh):
    return jax.shard_map(
        per_device,
        mesh=mesh,
        in_specs=(P("rows", "reg"), P("rows", "reg"), P("rows", None)),
        out_specs=(P("rows", "reg"), P("rows", None)),
        check_vma=False,
    )
```

profile of v0, /device:TPU:0, one launch (start us, length us, event | category | flops | bytes accessed | tf_op | source)
XLA Modules:
  0.0 394.9 jit_solution(7418192910360525687)
XLA Ops:
  7.2 1.5 copy-done
  8.8 4.6 %fusion.2 = f32[128,256]{0,1:T(8,128)} fusion(bf16[8192,128]{1,0:T(8,128)(2,1)S(1)} %copy-done, bf16[8192,256]{1,0:T(8,128)(2,1)} %param.7), kind=kOutput, calls=%fused_computation.9 | convolution fusion | flops 536870912 | bytes 6422528 | tf_op jit(solution)/shard_map/nr,nt->rt/dot_general | solution.py:28
  13.4 0.0 all-gather.5.cloned.1.call-start
  13.5 63.4 %reduce-scatter.2.cloned.1.call-done = f32[128,16]{0,1:T(8,128)} async-done(((f32[128,256]{0,1:T(8,128)}), f32[128,16]{0,1:T(8,128)}) %reduce-scatter.2.cloned.1.call-update) | async-done | bytes 8208 | tf_op jit(solution)/shard_map/reduce_scatter | solution.py:31
  76.9 0.8 copy.22
  77.7 16.4 %gather_fusion.1 = f32[8256,16]{1,0:T(8,128)} fusion(f32[128,16]{1,0:T(8,128)S(1)} %copy.22, s32[9216]{0:T(1024)S(1)} %pad_clamp_fusion), kind=kCustom, calls=%fused_computation.1.clone | custom fusion | bytes 1089792 | tf_op jit(solution)/shard_map/jit(_take)/gather | solution.py:10
  94.1 16.3 %gather_fusion = f32[8256,16]{1,0:T(8,128)} fusion(f32[128,16]{1,0:T(8,128)S(1)} %copy.22, s32[9216]{0:T(1024)S(1)} %pad_clamp_fusion.1), kind=kCustom, calls=%fused_computation.clone | custom fusion | bytes 1089792 | tf_op jit(solution)/shard_map/jit(_take)/gather | solution.py:10
  110.4 4.8 %mul.3 = bf16[8256,16]{1,0:T(8,128)(2,1)} multiply(f32[8256,16]{1,0:T(8,128)} %gather_fusion, f32[8256,16]{1,0:T(8,128)} %gather_fusion.1) | non-fusion elementwise | flops 132096 | bytes 1320960 | tf_op jit(solution)/shard_map/mul | solution.py:10
  115.1 2.1 copy.24
  117.3 0.7 maximum_convert_fusion
  118.0 1.4 convert_element_type.11
  119.4 0.8 copy.25
  120.2 3.5 all-to-all-start
  123.8 3.0 fusion.3
  126.8 57.9 %all-reduce.4 = bf16[128,256]{1,0:T(8,128)(2,1)S(1)} all-reduce(f32[128,256]{1,0:T(8,128)S(1)} %fusion.3), channel_id=1, replica_groups=mesh['rows'=16,'reg'=8] {'rows'}, use_global_device_ids=true, to_apply=%region_1.3 | all-reduce | flops 32768 | bytes 196608 | tf_op jit(solution)/shard_map/psum | solution.py:32
  184.7 1.0 fusion.4
  185.7 6.5 %copy.26 = bf16[8384,256]{1,0:T(8,128)(2,1)} copy(bf16[8384,256]{0,1:T(8,128)(2,1)} %all-gather.5.cloned.1.call-done) | data formatting | bytes 8585216 | tf_op jit(solution)/shard_map/all_gather | solution.py:35
  192.3 6.8 %all-to-all-start.1 = ((bf16[8,1048,256]{2,1,0:T(8,128)(2,1)}), bf16[8,1048,256]{2,1,0:T(8,128)(2,1)}, u32[]{:S(2)}, u32[]{:S(2)}) async-start(bf16[8,1048,256]{2,1,0:T(8,128)(2,1)} %bitcast.17), calls=%async_computation.2 | async-start | bytes 8585216 | tf_op jit(solution)/shard_map/all_to_all | solution.py:36
  199.1 0.5 all-gather.3.cloned.1.call-update
  199.7 119.2 %all-reduce.3.cloned.1.call-done = f32[524,128]{1,0:T(8,128)} async-done(((f32[524,128]{1,0:T(8,128)}), f32[524,128]{1,0:T(8,128)}) %all-reduce.3.cloned.1.call-update) | async-done | bytes 268304 | tf_op jit(solution)/shard_map/psum | solution.py:42
  318.9 1.7 broadcast_multiply_fusion
  320.6 4.8 %copy.28 = bf16[8,131,8,256]{3,2,0,1:T(8,128)(2,1)} copy(bf16[8,131,8,256]{3,2,1,0:T(8,128)(2,1)} %bitcast.5) | data formatting | bytes 8585216 | tf_op jit(solution)/shard_map/all_to_all | solution.py:36
  325.4 54.9 %all-gather.3.cloned.1.call-done = bf16[524,2048]{0,1:T(8,128)(2,1)} async-done(((bf16[524,256]{0,1:T(8,128)(2,1)}), bf16[524,2048]{0,1:T(8,128)(2,1)}) %all-gather.3.cloned.1.call-update) | async-done | bytes 2146320 | tf_op jit(solution)/shard_map/all_gather | solution.py:37
  380.4 8.0 %convolution_multiply_fusion = f32[524,1048]{1,0:T(8,128)} fusion(bf16[524,2048]{0,1:T(8,128)(2,1)} %all-gather.3.cloned.1.call-done, bf16[1048,2048]{1,0:T(8,128)(2,1)} %bitcast.18), kind=kOutput, calls=%fused_computation.2 | convolution fusion | flops 2249875712 | bytes 8635520 | tf_op jit(solution)/shard_map/dot_general | solution.py:16
  (20 shorter events, 0.2 us)
Async XLA Ops:
  7.2 1.6 copy-start
  7.2 6.2 %copy-start.2 = (s32[8256]{0:T(1024)S(1)}, s32[8256]{0:T(1024)}, u32[]{:S(2)}) copy-start(s32[8256]{0:T(1024)} %constant.39) | copy-start | bytes 99076
  7.2 6.3 %copy-start.3 = (s32[8256]{0:T(1024)S(1)}, s32[8256]{0:T(1024)}, u32[]{:S(2)}) copy-start(s32[8256]{0:T(1024)} %constant.40) | copy-start | bytes 99076
  7.2 69.7 %reduce-scatter.2.cloned.1.call-start = ((), (), s32[]{:S(2)}) async-start(), calls=%async_computation.3 | async-start | bytes 139264 | tf_op jit(solution)/shard_map/reduce_scatter | solution.py:31
  13.4 172.4 %all-gather.5.cloned.1.call-start = ((), (), s32[]{:S(2)}) async-start(), calls=%async_computation.5 | async-start | bytes 4595712 | tf_op jit(solution)/shard_map/all_gather | solution.py:35
  110.4 6.9 %copy-start.4 = (f32[128,16]{0,1:T(8,128)S(1)}, f32[128,16]{0,1:T(8,128)}, u32[]{:S(2)}) copy-start(f32[128,16]{0,1:T(8,128)} %reduce-scatter.2.cloned.1.call-done) | copy-start | bytes 24580
  120.2 64.5 %all-to-all-start = ((bf16[16,524,16]{1,2,0:T(8,128)(2,1)}), bf16[16,524,16]{1,2,0:T(8,128)(2,1)S(1)}, u32[]{:S(2)}, u32[]{:S(2)}) async-start(bf16[16,524,16]{1,2,0:T(8,128)(2,1)} %copy.25), calls=%async_computation.1 | async-start | bytes 655360 | tf_op jit(solution)/shard_map/all_to_all | solution.py:34
  123.8 195.2 %all-reduce.3.cloned.1.call-start = ((), (), s32[]{:S(2)}) async-start(), calls=%async_computation.6 | async-start | bytes 540672 | tf_op jit(solution)/shard_map/psum | solution.py:42
  184.7 7.6 %copy-start.1 = (bf16[16,524,16]{1,2,0:T(8,128)(2,1)}, bf16[16,524,16]{1,2,0:T(8,128)(2,1)S(1)}, u32[]{:S(2)}) copy-start(bf16[16,524,16]{1,2,0:T(8,128)(2,1)S(1)} %all-to-all-done) | copy-start | bytes 804868
  192.3 128.3 %all-to-all-start.1 = ((bf16[8,1048,256]{2,1,0:T(8,128)(2,1)}), bf16[8,1048,256]{2,1,0:T(8,128)(2,1)}, u32[]{:S(2)}, u32[]{:S(2)}) async-start(bf16[8,1048,256]{2,1,0:T(8,128)(2,1)} %bitcast.17), calls=%async_computation.2 | async-start | bytes 8585216 | tf_op jit(solution)/shard_map/all_to_all | solution.py:36
  199.1 181.3 %all-gather.3.cloned.1.call-start = ((), (), s32[]{:S(2)}) async-start(), calls=%async_computation.4 | async-start | bytes 2949120 | tf_op jit(solution)/shard_map/all_gather | solution.py:37
Sparse Core Ops, SparseCore 0:
  13.5 63.3 reduce-scatter.1
  118.1 38.6 all-gather.4
  185.8 133.0 all-reduce.2
  321.7 58.6 all-gather.2
where the time goes:
time: 396 us; the launch traced here: 395 us
  waiting for transfers between devices  238 us (60%)
  blocking collectives  57.9 us (15%)
  local copies, waits for them, and re-layouts  50.7 us (13%)
  matrix products  16.6 us (4%)
  between operations  13.9 us (4%)
  starting transfers between devices  10.5 us (3%)
  other arithmetic  7.18 us (2%)
    psum x1, waiting for transfers between devices, per_device(): rhs = lax.psum(rhs_part, 'reg')  119 us
    reduce_scatter x1, waiting for transfers between devices, per_device(): lax.psum_scatter(part_states, 'rows', scatter_dimension=1, tiled=True)  63.4 us
    psum x1, blocking collectives, per_device(): moments = lax.psum(part_rates, 'rows')  57.9 us
    all_gather x1, waiting for transfers between devices, per_device(): lax.all_gather(row_feat, 'reg', axis=1, tiled=True)  54.9 us
    gather x2, local copies, waits for them, and re-layouts, make_features(): quad = jnp.take(states, upper_i, axis=0) * jnp.take(states, upper_j, axis=0)  32.7 us
    dot_general x1, matrix products, block_adder(): lax.dot_general(piece, columns, (((1,), (1,)), ((), ())), preferred_eleme...  8.05 us
  transfers between devices with their start and end apart: 6, of which 3 were waited for; matrix products, arithmetic and copies ran while one was open for 5% of the time, Pallas kernels for 0%

commit v1 on v0

--- a/solution.py
+++ b/solution.py
@@ -3,6 +3,12 @@
 import numpy as np
 from jax import lax
 from jax.sharding import PartitionSpec as P
+
+
+def summed_here(array, axis):
+    blocks = lax.all_gather(array, axis, axis=0, tiled=False)
+    summed = blocks.sum(axis=0)
+    return summed
 
 
 def make_features(states):
@@ -39,7 +45,7 @@
     rhs_part = lax.dot_general(
         row_feat, rate_half, (((1,), (1,)), ((), ())), preferred_element_type=jnp.float32
     )
-    rhs = lax.psum(rhs_part, "reg")
+    rhs = summed_here(rhs_part, "reg")
     return (gram / float(total_time), rhs / float(total_time))
 
 

time: 396 us -> 359 us (0.907)
  waiting for transfers between devices: 238 us -> 201 us
    psum x1 -> x0, waiting for transfers between devices: 119 us -> none  [per_device(): rhs = lax.psum(rhs_part, 'reg')]
    all_gather x0 -> x1, waiting for transfers between devices: none -> 83.7 us  [summed_here(): blocks = lax.all_gather(array, axis, axis=0, tiled=False)]
  transfers between devices with their start and end apart: 6 -> 6, of which waited for: 3 -> 3; matrix products, arithmetic and copies ran while one was open for 5% -> 6% of each run, Pallas kernels for 0% -> 0%
where the time goes in v1:
time: 359 us; the launch traced here: 358 us
  waiting for transfers between devices  201 us (56%)
  blocking collectives  57.9 us (16%)
  local copies, waits for them, and re-layouts  50.7 us (14%)
  matrix products  16.6 us (5%)
  between operations  13.9 us (4%)
  starting transfers between devices  10.5 us (3%)
  other arithmetic  7.97 us (2%)
    all_gather x1, waiting for transfers between devices, summed_here(): blocks = lax.all_gather(array, axis, axis=0, tiled=False)  83.7 us
    reduce_scatter x1, waiting for transfers between devices, per_device(): lax.psum_scatter(part_states, 'rows', scatter_dimension=1, tiled=True)  63.4 us
    psum x1, blocking collectives, per_device(): moments = lax.psum(part_rates, 'rows')  57.9 us
    all_gather x1, waiting for transfers between devices, per_device(): lax.all_gather(row_feat, 'reg', axis=1, tiled=True)  53 us
    gather x2, local copies, waits for them, and re-layouts, make_features(): quad = jnp.take(states, upper_i, axis=0) * jnp.take(states, upper_j, axis=0)  32.7 us
    dot_general x1, matrix products, block_adder(): lax.dot_general(piece, columns, (((1,), (1,)), ((), ())), preferred_eleme...  8.05 us
  transfers between devices with their start and end apart: 6, of which 3 were waited for; matrix products, arithmetic and copies ran while one was open for 6% of the time, Pallas kernels for 0%

profile of v1, /device:TPU:0, one launch (start us, length us, event | category | flops | bytes accessed | tf_op | source)
XLA Modules:
  0.0 358.2 jit_solution(16580553196007981127)
XLA Ops:
  7.2 1.5 copy-done
  8.8 4.6 %fusion.1 = f32[128,256]{0,1:T(8,128)} fusion(bf16[8192,128]{1,0:T(8,128)(2,1)S(1)} %copy-done, bf16[8192,256]{1,0:T(8,128)(2,1)} %param.7), kind=kOutput, calls=%fused_computation.9 | convolution fusion | flops 536870912 | bytes 6422528 | tf_op jit(solution)/shard_map/nr,nt->rt/dot_general | solution.py:34
  13.5 63.4 %reduce-scatter.2.cloned.1.call-done = f32[128,16]{0,1:T(8,128)} async-done(((f32[128,256]{0,1:T(8,128)}), f32[128,16]{0,1:T(8,128)}) %reduce-scatter.2.cloned.1.call-update) | async-done | bytes 8208 | tf_op jit(solution)/shard_map/reduce_scatter | solution.py:37
  76.9 0.8 copy.22
  77.7 16.4 %gather_fusion.1 = f32[8256,16]{1,0:T(8,128)} fusion(f32[128,16]{1,0:T(8,128)S(1)} %copy.22, s32[9216]{0:T(1024)S(1)} %pad_clamp_fusion), kind=kCustom, calls=%fused_computation.1.clone | custom fusion | bytes 1089792 | tf_op jit(solution)/shard_map/jit(_take)/gather | solution.py:16
  94.1 16.3 %gather_fusion = f32[8256,16]{1,0:T(8,128)} fusion(f32[128,16]{1,0:T(8,128)S(1)} %copy.22, s32[9216]{0:T(1024)S(1)} %pad_clamp_fusion.1), kind=kCustom, calls=%fused_computation.clone | custom fusion | bytes 1089792 | tf_op jit(solution)/shard_map/jit(_take)/gather | solution.py:16
  110.4 4.8 %mul.3 = bf16[8256,16]{1,0:T(8,128)(2,1)} multiply(f32[8256,16]{1,0:T(8,128)} %gather_fusion, f32[8256,16]{1,0:T(8,128)} %gather_fusion.1) | non-fusion elementwise | flops 132096 | bytes 1320960 | tf_op jit(solution)/shard_map/mul | solution.py:16
  115.1 2.1 copy.24
  117.3 0.7 maximum_convert_fusion
  118.0 1.4 convert_element_type.11
  119.4 0.8 copy.25
  120.2 3.5 all-to-all-start
  123.8 3.0 fusion.2
  126.8 57.9 %all-reduce.1 = bf16[128,256]{1,0:T(8,128)(2,1)S(1)} all-reduce(f32[128,256]{1,0:T(8,128)S(1)} %fusion.2), channel_id=1, replica_groups=mesh['rows'=16,'reg'=8] {'rows'}, use_global_device_ids=true, to_apply=%region_1.3 | all-reduce | flops 32768 | bytes 196608 | tf_op jit(solution)/shard_map/psum | solution.py:38
  184.7 1.0 convolution_bitcast_fusion
  185.7 6.5 %copy.26 = bf16[8384,256]{1,0:T(8,128)(2,1)} copy(bf16[8384,256]{0,1:T(8,128)(2,1)} %all-gather.8.cloned.1.call-done) | data formatting | bytes 8585216 | tf_op jit(solution)/shard_map/all_gather | solution.py:41
  192.3 6.8 %all-to-all-start.1 = ((bf16[8,1048,256]{2,1,0:T(8,128)(2,1)}), bf16[8,1048,256]{2,1,0:T(8,128)(2,1)}, u32[]{:S(2)}, u32[]{:S(2)}) async-start(bf16[8,1048,256]{2,1,0:T(8,128)(2,1)} %bitcast.19), calls=%async_computation.2 | async-start | bytes 8585216 | tf_op jit(solution)/shard_map/all_to_all | solution.py:42
  199.1 0.5 all-gather.6.cloned.1.call-update
  199.7 83.7 %all-gather.10.cloned.1.call-done = f32[8,524,128]{2,1,0:T(8,128)} async-done(((f32[1,524,128]{2,1,0:T(8,128)}), f32[8,524,128]{2,1,0:T(8,128)}) %all-gather.10.cloned.1.call-update) | async-done | bytes 2146320 | tf_op jit(solution)/shard_map/all_gather | solution.py:9
  283.3 1.7 reduce_sum.9
  285.1 0.7 broadcast_multiply_fusion
  285.8 4.8 %copy.28 = bf16[8,131,8,256]{3,2,0,1:T(8,128)(2,1)} copy(bf16[8,131,8,256]{3,2,1,0:T(8,128)(2,1)} %bitcast.6) | data formatting | bytes 8585216 | tf_op jit(solution)/shard_map/all_to_all | solution.py:42
  290.6 53.0 %all-gather.6.cloned.1.call-done = bf16[524,2048]{0,1:T(8,128)(2,1)} async-done(((bf16[524,256]{0,1:T(8,128)(2,1)}), bf16[524,2048]{0,1:T(8,128)(2,1)}) %all-gather.6.cloned.1.call-update) | async-done | bytes 2146320 | tf_op jit(solution)/shard_map/all_gather | solution.py:43
  343.6 8.0 %convolution_multiply_fusion = f32[524,1048]{1,0:T(8,128)} fusion(bf16[524,2048]{0,1:T(8,128)(2,1)} %all-gather.6.cloned.1.call-done, bf16[1048,2048]{1,0:T(8,128)(2,1)} %bitcast.20), kind=kOutput, calls=%fused_computation.2 | convolution fusion | flops 2249875712 | bytes 8635520 | tf_op jit(solution)/shard_map/dot_general | solution.py:22
  (21 shorter events, 0.3 us)
Async XLA Ops:
  7.2 1.6 copy-start
  7.2 6.2 %copy-start.2 = (s32[8256]{0:T(1024)S(1)}, s32[8256]{0:T(1024)}, u32[]{:S(2)}) copy-start(s32[8256]{0:T(1024)} %constant.41) | copy-start | bytes 99076
  7.2 6.3 %copy-start.3 = (s32[8256]{0:T(1024)S(1)}, s32[8256]{0:T(1024)}, u32[]{:S(2)}) copy-start(s32[8256]{0:T(1024)} %constant.42) | copy-start | bytes 99076
  7.2 69.7 %reduce-scatter.2.cloned.1.call-start = ((), (), s32[]{:S(2)}) async-start(), calls=%async_computation.3 | async-start | bytes 139264 | tf_op jit(solution)/shard_map/reduce_scatter | solution.py:37
  13.4 172.4 %all-gather.8.cloned.1.call-start = ((), (), s32[]{:S(2)}) async-start(), calls=%async_computation.5 | async-start | bytes 4595712 | tf_op jit(solution)/shard_map/all_gather | solution.py:41
  110.4 6.9 %copy-start.4 = (f32[128,16]{0,1:T(8,128)S(1)}, f32[128,16]{0,1:T(8,128)}, u32[]{:S(2)}) copy-start(f32[128,16]{0,1:T(8,128)} %reduce-scatter.2.cloned.1.call-done) | copy-start | bytes 24580
  120.2 64.5 %all-to-all-start = ((bf16[16,524,16]{1,2,0:T(8,128)(2,1)}), bf16[16,524,16]{1,2,0:T(8,128)(2,1)S(1)}, u32[]{:S(2)}, u32[]{:S(2)}) async-start(bf16[16,524,16]{1,2,0:T(8,128)(2,1)} %copy.25), calls=%async_computation.1 | async-start | bytes 655360 | tf_op jit(solution)/shard_map/all_to_all | solution.py:40
  123.8 159.6 %all-gather.10.cloned.1.call-start = ((), (), s32[]{:S(2)}) async-start(), calls=%async_computation.6 | async-start | bytes 2433024 | tf_op jit(solution)/shard_map/all_gather | solution.py:9
  184.7 7.6 %copy-start.1 = (bf16[16,524,16]{1,2,0:T(8,128)(2,1)}, bf16[16,524,16]{1,2,0:T(8,128)(2,1)S(1)}, u32[]{:S(2)}) copy-start(bf16[16,524,16]{1,2,0:T(8,128)(2,1)S(1)} %all-to-all-done) | copy-start | bytes 804868
  192.3 93.5 %all-to-all-start.1 = ((bf16[8,1048,256]{2,1,0:T(8,128)(2,1)}), bf16[8,1048,256]{2,1,0:T(8,128)(2,1)}, u32[]{:S(2)}, u32[]{:S(2)}) async-start(bf16[8,1048,256]{2,1,0:T(8,128)(2,1)} %bitcast.19), calls=%async_computation.2 | async-start | bytes 8585216 | tf_op jit(solution)/shard_map/all_to_all | solution.py:42
  199.1 144.5 %all-gather.6.cloned.1.call-start = ((), (), s32[]{:S(2)}) async-start(), calls=%async_computation.4 | async-start | bytes 2949120 | tf_op jit(solution)/shard_map/all_gather | solution.py:43
Sparse Core Ops, SparseCore 0:
  13.5 63.3 reduce-scatter.1
  118.1 38.6 all-gather.7
  185.8 97.4 all-gather.9
  286.1 57.5 all-gather.5
